TPU v7x, 32 devices: a whole 2x2x4 slice. The times are simulated.
32 devices in a mesh: seq: 8 (over y, x, core), tp: 4 (over z).
Axes of the slice: x: 2, y: 2, z: 4, core: 2. Of those that a mesh axis runs over, the one named last changes fastest.
Arguments:
- projected: bfloat16 [1, 8192, 3, 4096], P(None, 'seq', None, 'tp'), may hold values from -6 to 6
- short_kernel: float32 [3, 3, 4096], P(None, None, 'tp'), may hold values from -3 to 3
- filters: float32 [2, 4096, 8192], P(None, ('tp', 'seq')), may hold values from -2 to 2
- skip_gain: float32 [2, 4096], P(None, ('tp', 'seq')), may hold values from -3 to 3
- out_weight: bfloat16 [4096, 4096], P('tp'), may hold values from -0.09375 to 0.09375
- out_grad: bfloat16 [1, 8192, 4096], P(None, 'seq', 'tp'), may hold values from -6 to 6
Outputs:
- output: bfloat16 [1, 8192, 4096], P(None, 'seq', 'tp')
- projected_grad: bfloat16 [1, 8192, 3, 4096], P(None, 'seq', None, 'tp')
- filter_grad: float32 [2, 4096, 8192], P(None, ('tp', 'seq'))
All inputs are finite; a program needn't handle non-finite values.
Results may differ from a plain program's by a relative error of at most 0.0095.
Values may be sent and summed in bfloat16 or wider, within the bound.
A program may use at most 384 MiB of HBM per device.

v0:
```python
import math
import jax
import jax.numpy as jnp
from jax import lax
from jax.sharding import PartitionSpec as P

LEN = 8192
SEQS = 1
precise = lax.Precision.HIGH


def from_behind(block, axis, distance):
    devices = range(lax.axis_size(axis))
    route = [(i - distance, i) for i in devices if i - distance in devices]
    return lax.ppermute(block, axis, route)


def dft_tables(length):
    total = 2 * length
    levels = total.bit_length() - 1
    outer = 2 ** (levels // 2)
    inner = total // outer
    halfway = outer // 2
    outer_ids = jnp.arange(outer, dtype=jnp.int32)
    inner_ids = jnp.arange(inner, dtype=jnp.int32)
    outer_angle = (outer_ids[:, None] * outer_ids[None, :] % outer).astype(jnp.float32) * (
        2.0 * math.pi / outer
    )
    outer_cos = jnp.cos(outer_angle)
    outer_sin = jnp.sin(outer_angle)
    opening = jnp.concatenate([outer_cos[:, :halfway], -outer_sin[:, :halfway]], axis=0)
    closing = jnp.concatenate([outer_cos[:halfway, :], -outer_sin[:halfway, :]], axis=1) / total
    inner_angle = (inner_ids[:, None] * inner_ids[None, :] % inner).astype(jnp.float32) * (
        2.0 * math.pi / inner
    )
    inner_cos = jnp.cos(inner_angle)
    inner_sin = jnp.sin(inner_angle)
    forward_mix = jnp.concatenate(
        [
            jnp.concatenate([inner_cos, -inner_sin], axis=1),
            jnp.concatenate([inner_sin, inner_cos], axis=1),
        ],
        axis=0,
    )
    inverse_mix = jnp.concatenate(
        [
            jnp.concatenate([inner_cos, inner_sin], axis=1),
            jnp.concatenate([-inner_sin, inner_cos], axis=1),
        ],
        axis=0,
    )
    twist_angle = (outer_ids[:, None] * inner_ids[None, :] % total).astype(jnp.float32) * (
        2.0 * math.pi / total
    )
    return (opening, closing, forward_mix, inverse_mix, jnp.cos(twist_angle), -jnp.sin(twist_angle))


def forward_dft(signal, tables):
    opening, closing, forward_mix, inverse_mix, twist_real, twist_imag = tables
    outer, inner = twist_real.shape
    row_count = signal.shape[0]
    shaped = signal.reshape(row_count, outer // 2, inner)
    mixed = jnp.einsum("kn,rnm->rkm", opening, shaped, precision=precise)
    real_part = mixed[:, :outer]
    imag_part = mixed[:, outer:]
    turned = jnp.concatenate(
        [
            real_part * twist_real - imag_part * twist_imag,
            real_part * twist_imag + imag_part * twist_real,
        ],
        axis=2,
    )
    spectrum = jnp.dot(turned.reshape(row_count * outer, 2 * inner), forward_mix, precision=precise)
    return spectrum.reshape(row_count, outer, 2 * inner)


def inverse_dft(spectrum, tables):
    opening, closing, forward_mix, inverse_mix, twist_real, twist_imag = tables
    outer, inner = twist_real.shape
    row_count = spectrum.shape[0]
    reverted = jnp.dot(
        spectrum.reshape(row_count * outer, 2 * inner), inverse_mix, precision=precise
    )
    reverted = reverted.reshape(row_count, outer, 2 * inner)
    real_part = reverted[..., :inner]
    imag_part = reverted[..., inner:]
    turned = jnp.concatenate(
        [
            real_part * twist_real + imag_part * twist_imag,
            imag_part * twist_real - real_part * twist_imag,
        ],
        axis=1,
    )
    signal = jnp.einsum("nk,rkm->rnm", closing, turned, precision=precise)
    return signal.reshape(row_count, -1)


def forward_rows(signal, tables):
    lead = signal.shape[:-1]
    flat_spec = forward_dft(signal.reshape(-1, signal.shape[-1]), tables)
    return flat_spec.reshape(lead + flat_spec.shape[1:])


def inverse_rows(spectrum, tables):
    lead = spectrum.shape[:-2]
    flat_signal = inverse_dft(spectrum.reshape((-1,) + spectrum.shape[-2:]), tables)
    return flat_signal.reshape(lead + (flat_signal.shape[-1],))


def spectral_product(left, right, conjugate):
    inner = left.shape[-1] // 2
    left_real = left[..., :inner]
    left_imag = -left[..., inner:] if conjugate else left[..., inner:]
    right_real = right[..., :inner]
    right_imag = right[..., inner:]
    return jnp.concatenate(
        [
            left_real * right_real - left_imag * right_imag,
            left_real * right_imag + left_imag * right_real,
        ],
        axis=-1,
    )


def edge_frames(block, shift_by):
    return from_behind(block, "seq", shift_by)


def to_channels(block):
    moved = lax.all_to_all(block, "seq", split_axis=3, concat_axis=2, tiled=True)
    return jnp.swapaxes(moved, 2, 3)


def to_frames(block):
    return lax.all_to_all(jnp.swapaxes(block, 2, 3), "seq", split_axis=2, concat_axis=3, tiled=True)


def local(projected, short_kernel, filters, skip_gain, out_weight, out_grad):
    seq_count, frames, _, local_width = projected.shape
    tables = dft_tables(LEN)
    edge_rows = edge_frames(projected[:, frames - 2 :], 1)
    padded = jnp.concatenate([edge_rows, projected], axis=1).astype(jnp.float32)
    short = sum(
        (
            short_kernel[:, offset, :] * padded[:, 2 - offset : 2 - offset + frames]
            for offset in range(3)
        )
    ).astype(jnp.bfloat16)
    outgoing = jnp.transpose(short, (2, 0, 1, 3))
    channel = to_channels(outgoing)
    short_v = channel[0].astype(jnp.float32)
    short_x1 = channel[1].astype(jnp.float32)
    gain_zero = skip_gain[0][None, :, None]
    gain_one = skip_gain[1][None, :, None]
    spec_zero = forward_rows(filters[0], tables)[None]
    spec_one = forward_rows(filters[1], tables)[None]
    spec_short = forward_rows(short_v, tables)
    first_conv = gain_zero * short_v + inverse_rows(
        spectral_product(spec_short, spec_zero, False), tables
    )
    middle = short_x1 * first_conv
    spec_middle = forward_rows(middle, tables)
    second = (
        gain_one * middle + inverse_rows(spectral_product(spec_middle, spec_one, False), tables)
    ).astype(jnp.bfloat16)
    short_x2 = channel[2].astype(jnp.float32)
    returned = (short_x2 * second.astype(jnp.float32)).astype(jnp.bfloat16)
    arrived = to_frames(returned[None])[0]
    flat_gated = arrived.reshape(seq_count * frames, local_width)
    summed = lax.psum_scatter(
        lax.dot_general(
            out_weight, flat_gated, (((0,), (1,)), ((), ())), preferred_element_type=jnp.float32
        ).astype(jnp.bfloat16),
        "tp",
        scatter_dimension=0,
        tiled=True,
    ).astype(jnp.float32)
    output = jnp.transpose(summed).reshape(seq_count, frames, local_width).astype(jnp.bfloat16)
    back_gated = lax.dot_general(
        lax.all_gather(out_grad, "tp", axis=2, tiled=True),
        out_weight,
        (((2,), (1,)), ((), ())),
        preferred_element_type=jnp.float32,
    ).astype(jnp.bfloat16)
    received = to_channels(back_gated[None])[0]
    back_gated_chan = received.astype(jnp.float32)
    back_second = (back_gated_chan * short_x2).astype(jnp.bfloat16).astype(jnp.float32)
    back_x2 = (back_gated_chan * second.astype(jnp.float32)).astype(jnp.bfloat16)
    spec_back_sec = forward_rows(back_second, tables)
    back_middle = gain_one * back_second + inverse_rows(
        spectral_product(spec_one, spec_back_sec, True), tables
    )
    grad_one = inverse_rows(
        jnp.sum(spectral_product(spec_middle, spec_back_sec, True), axis=0), tables
    )
    back_x1 = (back_middle * first_conv).astype(jnp.bfloat16)
    back_first = back_middle * short_x1
    spec_back_first = forward_rows(back_first, tables)
    back_v = (
        gain_zero * back_first
        + inverse_rows(spectral_product(spec_zero, spec_back_first, True), tables)
    ).astype(jnp.bfloat16)
    grad_zero = inverse_rows(
        jnp.sum(spectral_product(spec_short, spec_back_first, True), axis=0), tables
    )
    filter_grad = jnp.stack([grad_zero, grad_one]) * (SEQS * LEN) ** (-0.5)
    grads_chan = jnp.stack([back_v, back_x1, back_x2])
    grads_frames = jnp.transpose(to_frames(grads_chan), (1, 2, 0, 3))
    next_rows = edge_frames(grads_frames[:, :2], -1)
    tail = jnp.concatenate([grads_frames, next_rows], axis=1).astype(jnp.float32)
    projected_grad = sum(
        (short_kernel[:, offset, :] * tail[:, offset : offset + frames] for offset in range(3))
    ).astype(jnp.bfloat16)
    return (output, projected_grad, filter_grad)


def solution(mesh):
    in_specs = (
        P(None, "seq", None, "tp"),
        P(None, None, "tp"),
        P(None, ("tp", "seq"), None),
        P(None, ("tp", "seq")),
        P("tp", None),
        P(None, "seq", "tp"),
    )
    out_specs = (P(None, "seq", "tp"), P(None, "seq", None, "tp"), P(None, ("tp", "seq"), None))
    return jax.shard_map(local, mesh=mesh, in_specs=in_specs, out_specs=out_specs, check_vma=False)
```

profile of v0, /device:TPU:1, one launch (start us, length us, event | category | flops | bytes accessed | tf_op | source)
XLA Modules:
  0.0 1164.1 jit_solution(14599692841856185292)
XLA Ops:
  35.0 21.4 %fusion.92 = bf16[3,1,1024,1024]{2,3,0,1:T(8,128)(2,1)} fusion(f32[1,1026,3,1024]{1,3,2,0:T(8,128)} %maximum_convert_fusion, f32[3,1024]{1,0:T(4,128)S(1)} %get-tuple-element.85, f32[3,1024]{1,0:T(4,128)S(1)} %get-tuple-element.86, f32[3,1024]{1,0:T(4,128)S(1)} %bitcast.207), kind=kLoop, calls=%fused_computation.138 | loop fusion | flops 18874368 | bytes 44077056 | tf_op jit(solution)/shard_map/transpose | solution.py:149
  100.5 61.5 %all-to-all-done = bf16[3,1,1024,1024]{2,0,1,3:T(4,128)(2,1)} async-done(((bf16[3,1,1024,1024]{2,0,1,3:T(4,128)(2,1)}), bf16[3,1,1024,1024]{2,0,1,3:T(4,128)(2,1)}, u32[]{:S(2)}, u32[]{:S(2)}) %all-to-all-start) | async-done | bytes 6291488 | tf_op jit(solution)/shard_map/all_to_all | solution.py:130
  282.1 25.6 %multiply_subtract_fusion.9 = (f32[128,128,128]{1,2,0:T(8,128)}, f32[128,128,128]{1,2,0:T(8,128)}, f32[128,128,128]{1,2,0:T(8,128)}, f32[128,128,128]{1,2,0:T(8,128)}) fusion(f32[128,256,128]{1,2,0:T(8,128)} %convolution_bitcast_fusion.1, f32[128,128]{0,1:T(8,128)S(1)} %copy.407, f32[128,128]{0,1:T(8,128)S(1)} %copy.406, ...), kind=kLoop, calls=%fused_computation.118 | loop fusion | flops 25165824 | bytes 67239936 | tf_op jit(solution)/shard_map/sub | solution.py:68
  307.8 20.6 %fusion.75 = f32[1,128,128,256]{3,2,1,0:T(8,128)} fusion(f32[128,128,128]{1,2,0:T(8,128)} %get-tuple-element.43, f32[128,128,128]{1,2,0:T(8,128)} %get-tuple-element.42, f32[128,128]{1,0:T(8,128)S(1)} %get-tuple-element.88, f32[128,128]{1,0:T(8,128)S(1)} %get-tuple-element.87, f32[128,128]{1,0:T(8,128)S(1)} %fusion.158), kind=kOutput, calls=%fused_computation.85 | convolution fusion | flops 6446841856 | bytes 33751040 | tf_op jit(solution)/shard_map/dot_general | solution.py:73
  328.4 20.3 %fusion.78 = f32[1,128,128,256]{3,2,1,0:T(8,128)} fusion(f32[128,128,128]{1,2,0:T(8,128)} %get-tuple-element.78, f32[128,128,128]{1,2,0:T(8,128)} %get-tuple-element.79, f32[128,128]{1,0:T(8,128)S(1)} %get-tuple-element.88, f32[128,128]{1,0:T(8,128)S(1)} %get-tuple-element.87, f32[128,128]{1,0:T(8,128)S(1)} %fusion.158), kind=kOutput, calls=%fused_computation.86 | convolution fusion | flops 6446841856 | bytes 33751040 | tf_op jit(solution)/shard_map/dot_general | solution.py:73
  348.6 18.9 %multiply_subtract_fusion.8 = (f32[1,128,128,128]{3,2,1,0:T(8,128)}, f32[1,128,128,128]{3,2,1,0:T(8,128)}) fusion(f32[1,128,128,256]{3,2,1,0:T(8,128)} %fusion.75, f32[1,128,128,256]{3,2,1,0:T(8,128)} %fusion.78), kind=kLoop, calls=%fused_computation.116 | loop fusion | flops 14680064 | bytes 50331648 | tf_op jit(solution)/shard_map/sub | solution.py:118
  403.3 14.3 %convolution_bitcast_fusion = f32[128,256,128]{1,2,0:T(8,128)} fusion(f32[128,64,128]{2,1,0:T(8,128)} %copy.481, f32[128,64,128]{2,1,0:T(8,128)} %fusion.113, bf16[128,64,128]{2,1,0:T(8,128)(2,1)S(1)} %copy.485, f32[128]{0:T(128)S(1)} %copy-done.17, f32[128,64]{1,0:T(8,128)S(1)} %slice_negate_fusion, f32[128,64]{1,0:T(8,128)S(1)} %bitcast.192), kind=kOutput, calls=%fused_computation.90 | convolution fusion | flops 1614823424 | bytes 27329024 | tf_op jit(solution)/shard_map/kn,rnm->rkm/dot_general | solution.py:63
  417.7 32.0 %multiply_subtract_fusion.6 = (f32[128,128,128]{1,2,0:T(8,128)}, f32[128,128,128]{1,2,0:T(8,128)}, f32[128,128,128]{1,2,0:T(8,128)}, f32[128,128,128]{1,2,0:T(8,...) fusion(f32[128,256,128]{1,2,0:T(8,128)} %convolution_bitcast_fusion, f32[128,128]{0,1:T(8,128)S(1)} %copy.407, ...), kind=kLoop, calls=%fused_computation.112 | loop fusion | flops 37748736 | bytes 100794368 | tf_op jit(solution)/shard_map/sub | solution.py:68
  449.7 20.6 %fusion.72 = f32[1,128,128,256]{3,2,1,0:T(8,128)} fusion(f32[128,128,128]{1,2,0:T(8,128)} %get-tuple-element.39, f32[128,128,128]{1,2,0:T(8,128)} %get-tuple-element.38, f32[128,128]{1,0:T(8,128)S(1)} %get-tuple-element.88, f32[128,128]{1,0:T(8,128)S(1)} %get-tuple-element.87, f32[128,128]{1,0:T(8,128)S(1)} %fusion.158), kind=kOutput, calls=%fused_computation.84 | convolution fusion | flops 6446841856 | bytes 33751040 | tf_op jit(solution)/shard_map/dot_general | solution.py:73
  470.3 20.3 %fusion.84 = f32[1,128,128,256]{3,2,1,0:T(8,128)} fusion(f32[128,128,128]{1,2,0:T(8,128)} %get-tuple-element.74, f32[128,128,128]{1,2,0:T(8,128)} %get-tuple-element.75, f32[128,128]{1,0:T(8,128)S(1)} %get-tuple-element.88, f32[128,128]{1,0:T(8,128)S(1)} %get-tuple-element.87, f32[128,128]{1,0:T(8,128)S(1)} %fusion.158), kind=kOutput, calls=%fused_computation.88 | convolution fusion | flops 6446841856 | bytes 33751040 | tf_op jit(solution)/shard_map/dot_general | solution.py:73
  490.5 20.4 %fusion.87 = f32[1,128,128,256]{3,2,1,0:T(8,128)} fusion(f32[128,128,128]{1,2,0:T(8,128)} %get-tuple-element.76, f32[128,128,128]{1,2,0:T(8,128)} %get-tuple-element.77, f32[128,128]{1,0:T(8,128)S(1)} %get-tuple-element.88, f32[128,128]{1,0:T(8,128)S(1)} %get-tuple-element.87, f32[128,128]{1,0:T(8,128)S(1)} %fusion.158), kind=kOutput, calls=%fused_computation.89 | convolution fusion | flops 6446841856 | bytes 33751040 | tf_op jit(solution)/shard_map/dot_general | solution.py:73
  510.9 18.9 %multiply_subtract_fusion.5 = (f32[1,128,128,128]{3,2,1,0:T(8,128)}, f32[1,128,128,128]{3,2,1,0:T(8,128)}) fusion(f32[1,128,128,256]{3,2,1,0:T(8,128)} %fusion.72, f32[1,128,128,256]{3,2,1,0:T(8,128)} %fusion.84), kind=kLoop, calls=%fused_computation.110 | loop fusion | flops 14680064 | bytes 50331648 | tf_op jit(solution)/shard_map/sub | solution.py:118
  529.8 30.9 %multiply_subtract_fusion.3 = (f32[1,128,128,128]{3,2,1,0:T(8,128)}, f32[1,128,128,128]{3,2,1,0:T(8,128)}, f32[1,128,128,128]{3,2,1,0:T(8,128)}, f32[1,128,128,128]{3,2,1,0:T(8,128)}) fusion(f32[1,128,128,256]{3,2,1,0:T(8,128)} %fusion.72, f32[1,128,128,256]{3,2,1,0:T(8,128)} %fusion.87, f32[1,128,128,256]{3,2,1,0:T(8,128)} %fusion.84), kind=kLoop, calls=%fused_computation.106 | loop fusion | flops 27262976 | bytes 83886080 | tf_op jit(solution)/shard_map/sub | solution.py:118
  560.7 14.3 %fusion.45 = f32[128,128,256]{1,2,0:T(8,128)} fusion(f32[1,128,128,128]{3,2,1,0:T(8,128)} %get-tuple-element.25, f32[1,128,128,128]{3,2,1,0:T(8,128)} %get-tuple-element.24, f32[128,128]{1,0:T(8,128)S(1)} %get-tuple-element.88, f32[128,128]{1,0:T(8,128)S(1)} %fusion.158, f32[128,128]{1,0:T(8,128)S(1)} %get-tuple-element.87), kind=kOutput, calls=%fused_computation.49 | convolution fusion | flops 6446841856 | bytes 33751040 | tf_op jit(solution)/shard_map/dot_general | solution.py:81
  601.9 31.7 %multiply_add_fusion.2 = (f32[128,128,128]{1,2,0:T(8,128)}, f32[128,128,128]{1,2,0:T(8,128)}, f32[128,128,128]{1,2,0:T(8,128)}, f32[128,128,128]{1,2,0:T(8,128)}...) fusion(f32[128,128,256]{1,2,0:T(8,128)} %fusion.52, f32[128,128]{0,1:T(8,128)S(1)} %copy.407, ...), kind=kLoop, calls=%fused_computation.104 | loop fusion | flops 37748736 | bytes 100794368 | tf_op jit(solution)/shard_map/add | solution.py:89
  688.2 20.1 %fusion.81 = f32[1,128,128,256]{3,2,1,0:T(8,128)} fusion(f32[128,128,128]{1,2,0:T(8,128)} %get-tuple-element.47, f32[128,128,128]{1,2,0:T(8,128)} %get-tuple-element.46, f32[128,128]{1,0:T(8,128)S(1)} %get-tuple-element.88, f32[128,128]{1,0:T(8,128)S(1)} %get-tuple-element.87, f32[128,128]{1,0:T(8,128)S(1)} %fusion.158), kind=kOutput, calls=%fused_computation.87 | convolution fusion | flops 6446841856 | bytes 33751040 | tf_op jit(solution)/shard_map/dot_general | solution.py:73
  708.3 30.8 %multiply_subtract_fusion.1 = (f32[1,128,128,128]{3,2,1,0:T(8,128)}, f32[1,128,128,128]{3,2,1,0:T(8,128)}, f32[1,128,128,128]{3,2,1,0:T(8,128)}, f32[1,128,128,128]{3,2,1,0:T(8,128)}) fusion(f32[1,128,128,256]{3,2,1,0:T(8,128)} %fusion.75, f32[1,128,128,256]{3,2,1,0:T(8,128)} %fusion.81, f32[1,128,128,256]{3,2,1,0:T(8,128)} %fusion.78), kind=kLoop, calls=%fused_computation.102 | loop fusion | flops 27262976 | bytes 83886080 | tf_op jit(solution)/shard_map/sub | solution.py:118
  766.4 22.5 %multiply_add_fusion = (f32[128,128,128]{1,2,0:T(8,128)}, f32[128,128,128]{1,2,0:T(8,128)}, f32[128,128,128]{1,2,0:T(8,128)S(1)}, f32[128,128,128]{1,2,0:T(8,128)}) fusion(f32[128,128,256]{1,2,0:T(8,128)} %fusion.59, f32[128,128]{0,1:T(8,128)S(1)} %copy.407, f32[128,128]{0,1:T(8,128)S(1)} %copy.406, f32[128,128,256]{1,2,0:T(8,128)} %fusion.23), kind=kLoop, calls=%fused_computation.100 | loop fusion | flops 25165824 | bytes 67239936 | tf_op jit(solution)/shard_map/add | solution.py:89
  820.2 33.3 %copy.501 = bf16[1,1,8192,128]{3,1,0,2:T(2,128)(2,1)} copy(bf16[1,1,8192,128]{3,2,0,1:T(8,128)(2,1)S(1)} %fusion.122) | data formatting | bytes 4194304 | tf_op jit(solution)/shard_map/transpose | solution.py:135
  853.4 45.1 %reduce.1 = bf16[8192,128]{1,0:T(8,128)(2,1)S(1)} reduce(bf16[8192,1,1,128]{3,2,1,0:T(2,128)(2,1)} %bitcast.200, bf16[]{:T(256)} %broadcast.130), dimensions={1,2}, to_apply=%bitcast.174.reduce_sub_computation | reduce | bytes 4194306
  901.7 32.6 %all_to_all.63 = bf16[8,2,65536]{2,1,0:T(2,128)(2,1)S(1)} all-to-all(bf16[8,2,65536]{2,1,0:T(2,128)(2,1)} %reshape.355), channel_id=1, replica_groups=mesh['seq'=8,'tp'=4] {'seq'}, dimensions={0} | all-to-all | bytes 4194304 | tf_op jit(solution)/shard_map/all_to_all | solution.py:135
  943.7 14.9 %convert_bitcast_fusion = bf16[4096,1024]{0,1:T(8,128)(2,1)} fusion(bf16[1024,1024]{0,1:T(8,128)(2,1)} %bitcast.206, bf16[1024,4096]{1,0:T(8,128)(2,1)} %param.10), kind=kOutput, calls=%fused_computation.119 | convolution fusion | flops 8594128896 | bytes 18874368 | tf_op jit(solution)/shard_map/dot_general | solution.py:171
  963.4 40.0 %copy.441 = bf16[3,1,8192,128]{3,0,1,2:T(4,128)(2,1)} copy(bf16[3,1,8192,128]{3,2,0,1:T(8,128)(2,1)S(1)} %maximum_bitcast_fusion.12) | data formatting | bytes 12582912 | tf_op jit(solution)/shard_map/transpose | solution.py:135
  1045.6 54.8 %all-to-all-done.3 = bf16[3,1,8192,128]{3,0,1,2:T(4,128)(2,1)} async-done(((bf16[3,1,8192,128]{3,0,1,2:T(4,128)(2,1)}), bf16[3,1,8192,128]{3,0,1,2:T(4,128)(2,1)}, u32[]{:S(2)}, u32[]{:S(2)}) %all-to-all-start.3) | async-done | bytes 6291488 | tf_op jit(solution)/shard_map/all_to_all | solution.py:135
  (136 shorter events, 483.9 us)
Async XLA Ops:
  7.2 172.1 %all-gather.2.cloned.1.call-start = ((), (), s32[]{:S(2)}) async-start(), calls=%async_computation.6 | async-start | bytes 10485760 | tf_op jit(solution)/shard_map/all_gather | solution.py:180
  8.7 14.4 %collective-permute-start = (bf16[1,2,3,1024]{3,1,2,0:T(2,128)(2,1)S(1)}, bf16[1,2,3,1024]{3,1,2,0:T(2,128)(2,1)S(1)}, u32[]{:S(2)}, u32[]{:S(2)}) collective-permute-start(bf16[1,2,3,1024]{3,1,2,0:T(2,128)(2,1)S(1)} %slice.194), channel_id=1, source_target_pairs={{0,4},{4,8},{8,12},{12,16},{16,20},{20,24},{24,28},{1,5},{5,9},{9,... | collective-permute-start | bytes 36872 | tf_op jit(solution)/shard_map/ppermute | solution.py:15
  14.2 20.8 %copy-start.11 = (f32[3,1024]{1,0:T(4,128)}, f32[3,1024]{1,0:T(4,128)S(1)}, u32[]{:S(2)}) copy-start(f32[3,1024]{1,0:T(4,128)S(1)} %get-tuple-element.85) | copy-start | bytes 36868
  14.2 20.7 %copy-start.13 = (f32[3,1024]{1,0:T(4,128)}, f32[3,1024]{1,0:T(4,128)S(1)}, u32[]{:S(2)}) copy-start(f32[3,1024]{1,0:T(4,128)S(1)} %get-tuple-element.86) | copy-start | bytes 36868
  23.1 11.9 %copy-start.15 = (f32[3,1,1024]{2,0,1:T(4,128)}, f32[3,1,1024]{2,0,1:T(4,128)S(1)}, u32[]{:S(2)}) copy-start(f32[3,1,1024]{2,0,1:T(4,128)S(1)} %copy.500) | copy-start | bytes 36868
  67.9 94.1 %all-to-all-start = ((bf16[3,1,1024,1024]{2,0,1,3:T(4,128)(2,1)}), bf16[3,1,1024,1024]{2,0,1,3:T(4,128)(2,1)}, u32[]{:S(2)}, u32[]{:S(2)}) async-start(bf16[3,1,1024,1024]{2,0,1,3:T(4,128)(2,1)} %copy.401), calls=%async_computation | async-start | bytes 16777216 | tf_op jit(solution)/shard_map/all_to_all | solution.py:130
  81.1 307.7 %copy-start.9 = (f32[64,128]{1,0:T(8,128)}, f32[64,128]{1,0:T(8,128)S(1)}, u32[]{:S(2)}) copy-start(f32[64,128]{1,0:T(8,128)S(1)} %slice_negate_fusion.1) | copy-start | bytes 98308
  81.1 322.3 %copy-start.5 = (f32[128,64]{1,0:T(8,128)}, f32[128,64]{1,0:T(8,128)S(1)}, u32[]{:S(2)}) copy-start(f32[128,64]{1,0:T(8,128)S(1)} %slice_negate_fusion) | copy-start | bytes 98308
  217.7 30.6 %all-to-all-start.2 = ((bf16[8,2,65536]{2,1,0:T(2,128)(2,1)}), bf16[8,2,65536]{2,1,0:T(2,128)(2,1)}, u32[]{:S(2)}, u32[]{:S(2)}) async-start(bf16[8,2,65536]{2,1,0:T(2,128)(2,1)} %reshape.357), calls=%async_computation.3 | async-start | bytes 4194304 | tf_op jit(solution)/shard_map/all_to_all | solution.py:130
  225.1 932.0 %reduce-scatter.2.cloned.1.call-start = ((), (), s32[]{:S(2)}) async-start(), calls=%async_computation.5 | async-start | bytes 10485760 | tf_op jit(solution)/shard_map/reduce_scatter | solution.py:170
  234.0 14.3 %copy-start.1 = (bf16[128,64,128]{2,1,0:T(8,128)(2,1)}, bf16[128,64,128]{2,1,0:T(8,128)(2,1)S(1)}, u32[]{:S(2)}) copy-start(bf16[128,64,128]{2,1,0:T(8,128)(2,1)S(1)} %copy.477) | copy-start | bytes 6291460
  381.6 7.2 copy-start.7
  560.7 28.2 %slice-start = ((s8[8388608]{0:T(1024)(128)(4,1)}), s8[4194304]{0:T(1024)(128)(4,1)S(1)}, s32[]{:S(2)}) async-start(s8[8388608]{0:T(1024)(128)(4,1)} %bitcast.180), calls=%async_computation.7 | async-start | bytes 8388608
  575.0 13.8 %slice-start.1 = ((s8[8388608]{0:T(1024)(128)(4,1)}), s8[4194304]{0:T(1024)(128)(4,1)S(1)}, s32[]{:S(2)}) async-start(s8[8388608]{0:T(1024)(128)(4,1)} %bitcast.180), calls=%async_computation.8 | async-start | bytes 8388608
  601.9 31.7 %copy-start.8 = (f32[64,128]{1,0:T(8,128)S(1)}, f32[64,128]{1,0:T(8,128)}, u32[]{:S(2)}) copy-start(f32[64,128]{1,0:T(8,128)} %slice.271) | copy-start | bytes 98308
  601.9 31.7 %copy-start.10 = (f32[64,128]{1,0:T(8,128)S(1)}, f32[64,128]{1,0:T(8,128)}, u32[]{:S(2)}) copy-start(f32[64,128]{1,0:T(8,128)} %copy-done.9) | copy-start | bytes 98308
  664.6 5.6 copy-start.2
  664.6 5.6 copy-start.6
  664.6 5.6 copy-start.19
  739.1 14.3 %copy-start = (f32[1,128,128,128]{3,2,1,0:T(8,128)S(1)}, f32[1,128,128,128]{3,2,1,0:T(8,128)}, u32[]{:S(2)}) copy-start(f32[1,128,128,128]{3,2,1,0:T(8,128)} %get-tuple-element.58) | copy-start | bytes 25165828
  800.3 5.6 copy-start.3
  800.3 5.6 copy-start.18
  1003.4 97.0 %all-to-all-start.3 = ((bf16[3,1,8192,128]{3,0,1,2:T(4,128)(2,1)}), bf16[3,1,8192,128]{3,0,1,2:T(4,128)(2,1)}, u32[]{:S(2)}, u32[]{:S(2)}) async-start(bf16[3,1,8192,128]{3,0,1,2:T(4,128)(2,1)} %copy.441), calls=%async_computation.4 | async-start | bytes 16777216 | tf_op jit(solution)/shard_map/all_to_all | solution.py:135
  1117.6 13.6 %collective-permute-start.1 = (bf16[1,2,3,1024]{3,1,2,0:T(2,128)(2,1)S(1)}, bf16[1,2,3,1024]{3,1,2,0:T(2,128)(2,1)S(1)}, u32[]{:S(2)}, u32[]{:S(2)}) collective-permute-start(bf16[1,2,3,1024]{3,1,2,0:T(2,128)(2,1)S(1)} %copy.444), channel_id=1, source_target_pairs={{4,0},{8,4},{12,8},{16,12},{20,16},{24,20},{28,24},{5,1},{9,5},{13... | collective-permute-start | bytes 36872 | tf_op jit(solution)/shard_map/ppermute | solution.py:15
  (6 other events, 22.7 us)
Sparse Core Ops, SparseCore 0:
  9.5 151.8 all-gather.1
  958.8 144.7 reduce-scatter.1
where the time goes:
time: 1170 us; the launch traced here: 1160 us
  other arithmetic  369 us (32%)
  matrix products  366 us (31%)
  local copies, waits for them, and re-layouts  236 us (20%)
  waiting for transfers between devices  117 us (10%)
  blocking collectives  32.6 us (3%)
  starting transfers between devices  29.1 us (2%)
  between operations  14.6 us (1%)
    dot_general x6, matrix products, forward_dft(): jnp.dot(turned.reshape(row_count * outer, 2 * inner), forward_mix, precis...  122 us
    sub x4, other arithmetic, spectral_product(): left_real * right_real - left_imag * right_imag  99.5 us
    dot_general x6, matrix products, inverse_dft(): jnp.dot(spectrum.reshape(row_count * outer, 2 * inner), inverse_mix, prec...  82.5 us
    transpose x2, local copies, waits for them, and re-layouts, to_frames(): jnp.swapaxes(block, 2, 3)  73.3 us
    dot_general x6, matrix products, inverse_dft(): signal = jnp.einsum('nk,rkm->rnm', closing, turned, precision=precise)  71.7 us
    sub x3, other arithmetic, forward_dft(): real_part * twist_real - imag_part * twist_imag  64.9 us
    all_to_all x2, waiting for transfers between devices, to_channels(): lax.all_to_all(block, 'seq', split_axis=3, concat_axis=2, tiled=True)  61.5 us
    add x3, other arithmetic, inverse_dft(): real_part * twist_real + imag_part * twist_imag  61.3 us
  transfers between devices with their start and end apart: 7, of which 2 were waited for; matrix products, arithmetic and copies ran while one was open for 22% of the time, Pallas kernels for 0%

commit v1 on v0

--- a/solution.py
+++ b/solution.py
@@ -132,7 +132,15 @@
 
 
 def to_frames(block):
-    return lax.all_to_all(jnp.swapaxes(block, 2, 3), "seq", split_axis=2, concat_axis=3, tiled=True)
+    return jnp.concatenate(
+        lax.all_to_all(
+            jnp.stack(jnp.split(jnp.swapaxes(block, 2, 3), lax.axis_size("seq"), axis=2)),
+            "seq",
+            0,
+            0,
+        ),
+        axis=3,
+    )
 
 
 def local(projected, short_kernel, filters, skip_gain, out_weight, out_grad):

time: 1170 us -> 1060 us (0.906)
  local copies, waits for them, and re-layouts: 236 us -> 148 us
  waiting for transfers between devices: 117 us -> 98.4 us
    transpose x3 -> x0, local copies, waits for them, and re-layouts: 84.8 us -> none  [the longest x2 73.3 us: to_frames(): jnp.swapaxes(block, 2, 3)]
    all_gather x1, waiting for transfers between devices: 0.01 us -> 65 us  [local(): lax.all_gather(out_grad, 'tp', axis=2, tiled=True)]
    all_to_all x2, waiting for transfers between devices: 61.5 us -> 0.01 us  [to_channels(): lax.all_to_all(block, 'seq', split_axis=3, concat_axis=2, tiled=True)]
    unnamed x3, other arithmetic: 57.8 us -> 15.5 us
    all_to_all x1, waiting for transfers between devices: 54.8 us -> 32.7 us  [to_frames(): lax.all_to_all(jnp.stack(jnp.split(jnp.swapaxes(block, 2, 3), lax.axis_si...]
    convert_element_type x1, other arithmetic: 11.5 us -> 33 us  [local(): projected_grad = sum((short_kernel[:, offset, :] * tail[:, offset:offset...]
    all_to_all x3 -> x0, local copies, waits for them, and re-layouts: 18.3 us -> none  [to_frames(): lax.all_to_all(jnp.swapaxes(block, 2, 3), 'seq', split_axis=2, concat_axi...]
    unnamed x59 -> x75, local copies, waits for them, and re-layouts: 45.7 us -> 57.7 us
  transfers between devices with their start and end apart: 7 -> 7, of which waited for: 2 -> 2; matrix products, arithmetic and copies ran while one was open for 22% -> 27% of each run, Pallas kernels for 0% -> 0%
where the time goes in v1:
time: 1060 us; the launch traced here: 1050 us
  other arithmetic  367 us (35%)
  matrix products  367 us (35%)
  local copies, waits for them, and re-layouts  148 us (14%)
  waiting for transfers between devices  98.4 us (9%)
  blocking collectives  29.4 us (3%)
  starting transfers between devices  25.4 us (2%)
  between operations  14.7 us (1%)
    dot_general x6, matrix products, forward_dft(): jnp.dot(turned.reshape(row_count * outer, 2 * inner), forward_mix, precis...  122 us
    sub x4, other arithmetic, spectral_product(): left_real * right_real - left_imag * right_imag  99.5 us
    dot_general x6, matrix products, inverse_dft(): jnp.dot(spectrum.reshape(row_count * outer, 2 * inner), inverse_mix, prec...  82.2 us
    dot_general x6, matrix products, inverse_dft(): signal = jnp.einsum('nk,rkm->rnm', closing, turned, precision=precise)  75.9 us
    all_gather x1, waiting for transfers between devices, local(): lax.all_gather(out_grad, 'tp', axis=2, tiled=True)  65 us
    sub x3, other arithmetic, forward_dft(): real_part * twist_real - imag_part * twist_imag  64.8 us
    add x3, other arithmetic, inverse_dft(): real_part * twist_real + imag_part * twist_imag  63.8 us
    dot_general x6, matrix products, forward_dft(): mixed = jnp.einsum('kn,rnm->rkm', opening, shaped, precision=precise)  59.1 us
  transfers between devices with their start and end apart: 7, of which 2 were waited for; matrix products, arithmetic and copies ran while one was open for 27% of the time, Pallas kernels for 0%

profile of v1, /device:TPU:1, one launch (start us, length us, event | category | flops | bytes accessed | tf_op | source)
XLA Modules:
  0.0 1050.7 jit_solution(17683624733207946158)
XLA Ops:
  14.2 14.6 %copy.235 = bf16[1,1024,3,1024]{1,2,0,3:T(4,128)(2,1)} copy(bf16[1,1024,3,1024]{3,1,2,0:T(8,128)(2,1)} %param.6) | data formatting | bytes 12582912 | tf_op args[0]
  41.2 29.8 %fusion.92 = bf16[3,1,1024,1024]{2,0,1,3:T(4,128)(2,1)} fusion(f32[1,1026,3,1024]{1,2,0,3:T(4,128)} %maximum_convert_fusion, f32[3,1024]{0,1:T(8,128)S(1)} %bitcast.282, f32[3,1024]{0,1:T(8,128)S(1)} %bitcast.284, f32[3,1024]{0,1:T(8,128)S(1)} %bitcast.280), kind=kLoop, calls=%fused_computation.138 | loop fusion | flops 18874368 | bytes 44077056 | tf_op jit(solution)/shard_map/transpose | solution.py:157
  96.4 65.0 %all-gather.2.cloned.1.call-done = bf16[1,1024,4096]{2,1,0:T(8,128)(2,1)} async-done(((bf16[1,1024,1024]{2,1,0:T(8,128)(2,1)}), bf16[1,1024,4096]{2,1,0:T(8,128)(2,1)}) %all-gather.2.cloned.1.call-update) | async-done | bytes 8388624 | tf_op jit(solution)/shard_map/all_gather | solution.py:188
  289.6 25.6 %multiply_subtract_fusion.9 = (f32[128,128,128]{1,2,0:T(8,128)}, f32[128,128,128]{1,2,0:T(8,128)}, f32[128,128,128]{1,2,0:T(8,128)}, f32[128,128,128]{1,2,0:T(8,128)}) fusion(f32[128,256,128]{1,2,0:T(8,128)} %convolution_bitcast_fusion.1, f32[128,128]{0,1:T(8,128)S(1)} %copy.241, f32[128,128]{0,1:T(8,128)S(1)} %copy.240, ...), kind=kLoop, calls=%fused_computation.120 | loop fusion | flops 25165824 | bytes 67239936 | tf_op jit(solution)/shard_map/sub | solution.py:68
  315.2 20.2 %fusion.75 = f32[1,128,128,256]{3,2,1,0:T(8,128)} fusion(f32[128,128,128]{1,2,0:T(8,128)} %get-tuple-element.37, f32[128,128,128]{1,2,0:T(8,128)} %get-tuple-element.36, f32[128,128]{1,0:T(8,128)S(1)} %get-tuple-element.86, f32[128,128]{1,0:T(8,128)S(1)} %get-tuple-element.85, f32[128,128]{1,0:T(8,128)S(1)} %fusion.172), kind=kOutput, calls=%fused_computation.87 | convolution fusion | flops 6446841856 | bytes 33751040 | tf_op jit(solution)/shard_map/dot_general | solution.py:73
  335.4 20.3 %fusion.78 = f32[1,128,128,256]{3,2,1,0:T(8,128)} fusion(f32[128,128,128]{1,2,0:T(8,128)} %get-tuple-element.74, f32[128,128,128]{1,2,0:T(8,128)} %get-tuple-element.75, f32[128,128]{1,0:T(8,128)S(1)} %get-tuple-element.86, f32[128,128]{1,0:T(8,128)S(1)} %get-tuple-element.85, f32[128,128]{1,0:T(8,128)S(1)} %fusion.172), kind=kOutput, calls=%fused_computation.88 | convolution fusion | flops 6446841856 | bytes 33751040 | tf_op jit(solution)/shard_map/dot_general | solution.py:73
  355.7 18.9 %multiply_subtract_fusion.8 = (f32[1,128,128,128]{3,2,1,0:T(8,128)}, f32[1,128,128,128]{3,2,1,0:T(8,128)}) fusion(f32[1,128,128,256]{3,2,1,0:T(8,128)} %fusion.75, f32[1,128,128,256]{3,2,1,0:T(8,128)} %fusion.78), kind=kLoop, calls=%fused_computation.118 | loop fusion | flops 14680064 | bytes 50331648 | tf_op jit(solution)/shard_map/sub | solution.py:118
  374.6 14.2 %fusion.40 = f32[128,128,256]{1,2,0:T(8,128)} fusion(f32[1,128,128,128]{3,2,1,0:T(8,128)} %get-tuple-element.21, f32[1,128,128,128]{3,2,1,0:T(8,128)} %get-tuple-element.20, f32[128,128]{1,0:T(8,128)S(1)} %get-tuple-element.86, f32[128,128]{1,0:T(8,128)S(1)} %fusion.172, f32[128,128]{1,0:T(8,128)S(1)} %get-tuple-element.85), kind=kOutput, calls=%fused_computation.49 | convolution fusion | flops 6446841856 | bytes 33751040 | tf_op jit(solution)/shard_map/dot_general | solution.py:81
  427.8 32.0 %multiply_subtract_fusion.6 = (f32[128,128,128]{1,2,0:T(8,128)}, f32[128,128,128]{1,2,0:T(8,128)}, f32[128,128,128]{1,2,0:T(8,128)}, f32[128,128,128]{1,2,0:T(8,...) fusion(f32[128,256,128]{1,2,0:T(8,128)} %convolution_bitcast_fusion, f32[128,128]{0,1:T(8,128)S(1)} %copy.241, ...), kind=kLoop, calls=%fused_computation.114 | loop fusion | flops 37748736 | bytes 100794368 | tf_op jit(solution)/shard_map/sub | solution.py:68
  459.8 20.1 %fusion.72 = f32[1,128,128,256]{3,2,1,0:T(8,128)} fusion(f32[128,128,128]{1,2,0:T(8,128)} %get-tuple-element.33, f32[128,128,128]{1,2,0:T(8,128)} %get-tuple-element.32, f32[128,128]{1,0:T(8,128)S(1)} %get-tuple-element.86, f32[128,128]{1,0:T(8,128)S(1)} %get-tuple-element.85, f32[128,128]{1,0:T(8,128)S(1)} %fusion.172), kind=kOutput, calls=%fused_computation.86 | convolution fusion | flops 6446841856 | bytes 33751040 | tf_op jit(solution)/shard_map/dot_general | solution.py:73
  479.9 20.5 %fusion.84 = f32[1,128,128,256]{3,2,1,0:T(8,128)} fusion(f32[128,128,128]{1,2,0:T(8,128)} %get-tuple-element.70, f32[128,128,128]{1,2,0:T(8,128)} %get-tuple-element.71, f32[128,128]{1,0:T(8,128)S(1)} %get-tuple-element.86, f32[128,128]{1,0:T(8,128)S(1)} %get-tuple-element.85, f32[128,128]{1,0:T(8,128)S(1)} %fusion.172), kind=kOutput, calls=%fused_computation.90 | convolution fusion | flops 6446841856 | bytes 33751040 | tf_op jit(solution)/shard_map/dot_general | solution.py:73
  500.4 20.2 %fusion.87 = f32[1,128,128,256]{3,2,1,0:T(8,128)} fusion(f32[128,128,128]{1,2,0:T(8,128)} %get-tuple-element.72, f32[128,128,128]{1,2,0:T(8,128)} %get-tuple-element.73, f32[128,128]{1,0:T(8,128)S(1)} %get-tuple-element.86, f32[128,128]{1,0:T(8,128)S(1)} %get-tuple-element.85, f32[128,128]{1,0:T(8,128)S(1)} %fusion.172), kind=kOutput, calls=%fused_computation.91 | convolution fusion | flops 6446841856 | bytes 33751040 | tf_op jit(solution)/shard_map/dot_general | solution.py:73
  520.6 18.9 %multiply_subtract_fusion.5 = (f32[1,128,128,128]{3,2,1,0:T(8,128)}, f32[1,128,128,128]{3,2,1,0:T(8,128)}) fusion(f32[1,128,128,256]{3,2,1,0:T(8,128)} %fusion.72, f32[1,128,128,256]{3,2,1,0:T(8,128)} %fusion.84), kind=kLoop, calls=%fused_computation.112 | loop fusion | flops 14680064 | bytes 50331648 | tf_op jit(solution)/shard_map/sub | solution.py:118
  539.5 30.9 %multiply_subtract_fusion.3 = (f32[1,128,128,128]{3,2,1,0:T(8,128)}, f32[1,128,128,128]{3,2,1,0:T(8,128)}, f32[1,128,128,128]{3,2,1,0:T(8,128)}, f32[1,128,128,128]{3,2,1,0:T(8,128)}) fusion(f32[1,128,128,256]{3,2,1,0:T(8,128)} %fusion.72, f32[1,128,128,256]{3,2,1,0:T(8,128)} %fusion.87, f32[1,128,128,256]{3,2,1,0:T(8,128)} %fusion.84), kind=kLoop, calls=%fused_computation.108 | loop fusion | flops 27262976 | bytes 83886080 | tf_op jit(solution)/shard_map/sub | solution.py:118
  570.5 14.1 %fusion.51 = f32[128,128,256]{1,2,0:T(8,128)} fusion(f32[1,128,128,128]{3,2,1,0:T(8,128)} %get-tuple-element.19, f32[1,128,128,128]{3,2,1,0:T(8,128)} %get-tuple-element.18, f32[128,128]{1,0:T(8,128)S(1)} %get-tuple-element.86, f32[128,128]{1,0:T(8,128)S(1)} %fusion.172, f32[128,128]{1,0:T(8,128)S(1)} %get-tuple-element.85), kind=kOutput, calls=%fused_computation.61 | convolution fusion | flops 6446841856 | bytes 33751040 | tf_op jit(solution)/shard_map/dot_general | solution.py:81
  611.4 31.7 %multiply_add_fusion.2 = (f32[128,128,128]{1,2,0:T(8,128)}, f32[128,128,128]{1,2,0:T(8,128)}, f32[128,128,128]{1,2,0:T(8,128)}, f32[128,128,128]{1,2,0:T(8,128)}...) fusion(f32[128,128,256]{1,2,0:T(8,128)} %fusion.58, f32[128,128]{0,1:T(8,128)S(1)} %copy.241, ...), kind=kLoop, calls=%fused_computation.106 | loop fusion | flops 37748736 | bytes 100794368 | tf_op jit(solution)/shard_map/add | solution.py:89
  696.0 20.5 %fusion.81 = f32[1,128,128,256]{3,2,1,0:T(8,128)} fusion(f32[128,128,128]{1,2,0:T(8,128)} %get-tuple-element.41, f32[128,128,128]{1,2,0:T(8,128)} %get-tuple-element.40, f32[128,128]{1,0:T(8,128)S(1)} %get-tuple-element.86, f32[128,128]{1,0:T(8,128)S(1)} %get-tuple-element.85, f32[128,128]{1,0:T(8,128)S(1)} %fusion.172), kind=kOutput, calls=%fused_computation.89 | convolution fusion | flops 6446841856 | bytes 33751040 | tf_op jit(solution)/shard_map/dot_general | solution.py:73
  716.5 30.8 %multiply_subtract_fusion.1 = (f32[1,128,128,128]{3,2,1,0:T(8,128)}, f32[1,128,128,128]{3,2,1,0:T(8,128)}, f32[1,128,128,128]{3,2,1,0:T(8,128)}, f32[1,128,128,128]{3,2,1,0:T(8,128)}) fusion(f32[1,128,128,256]{3,2,1,0:T(8,128)} %fusion.75, f32[1,128,128,256]{3,2,1,0:T(8,128)} %fusion.81, f32[1,128,128,256]{3,2,1,0:T(8,128)} %fusion.78), kind=kLoop, calls=%fused_computation.104 | loop fusion | flops 27262976 | bytes 83886080 | tf_op jit(solution)/shard_map/sub | solution.py:118
  747.3 14.1 %fusion.65 = f32[128,128,256]{1,2,0:T(8,128)} fusion(f32[1,128,128,128]{3,2,1,0:T(8,128)} %get-tuple-element.17, f32[1,128,128,128]{3,2,1,0:T(8,128)} %get-tuple-element.16, f32[128,128]{1,0:T(8,128)S(1)} %get-tuple-element.86, f32[128,128]{1,0:T(8,128)S(1)} %fusion.172, f32[128,128]{1,0:T(8,128)S(1)} %get-tuple-element.85), kind=kOutput, calls=%fused_computation.77 | convolution fusion | flops 6446841856 | bytes 33751040 | tf_op jit(solution)/shard_map/dot_general | solution.py:81
  774.3 22.5 %multiply_add_fusion = (f32[128,128,128]{1,2,0:T(8,128)}, f32[128,128,128]{1,2,0:T(8,128)}, f32[128,128,128]{1,2,0:T(8,128)S(1)}, f32[128,128,128]{1,2,0:T(8,128)}) fusion(f32[128,128,256]{1,2,0:T(8,128)} %fusion.65, f32[128,128]{0,1:T(8,128)S(1)} %copy.241, f32[128,128]{0,1:T(8,128)S(1)} %copy.240, f32[128,128,256]{1,2,0:T(8,128)} %fusion.29), kind=kLoop, calls=%fused_computation.102 | loop fusion | flops 25165824 | bytes 67239936 | tf_op jit(solution)/shard_map/add | solution.py:89
  828.3 29.4 %all_to_all.40 = bf16[8,1,1,1024,128]{3,4,2,1,0:T(8,128)(2,1)S(1)} all-to-all(bf16[8,1,1,1024,128]{3,4,2,1,0:T(8,128)(2,1)S(1)} %fusion.137), channel_id=1, replica_groups=mesh['seq'=8,'tp'=4] {'seq'}, dimensions={0} | all-to-all | bytes 4194304 | tf_op jit(solution)/shard_map/all_to_all | solution.py:136
  857.6 14.6 %convert_bitcast_fusion = bf16[4096,1024]{0,1:T(8,128)(2,1)} fusion(bf16[1024,1024]{0,1:T(8,128)(2,1)S(1)} %bitcast.286, bf16[1024,4096]{1,0:T(8,128)(2,1)} %param.10), kind=kOutput, calls=%fused_computation.121 | convolution fusion | flops 8594128896 | bytes 18874368 | tf_op jit(solution)/shard_map/dot_general | solution.py:179
  926.5 32.7 %all-to-all-done.3 = bf16[8,3,1,1024,128]{3,4,1,2,0:T(8,128)(2,1)} async-done(((bf16[8,3,1,1024,128]{3,4,1,2,0:T(8,128)(2,1)}), bf16[8,3,1,1024,128]{3,4,1,2,0:T(8,128)(2,1)}, u32[]{:S(2)}, u32[]{:S(2)}) %all-to-all-start.3) | async-done | bytes 6291488 | tf_op jit(solution)/shard_map/all_to_all | solution.py:136
  997.6 33.0 %fusion.1 = bf16[1,1024,3,1024]{1,2,0,3:T(4,128)(2,1)} fusion(f32[1,1026,3,1024]{1,2,0,3:T(4,128)} %maximum_convert_fusion.1, f32[3,1024]{0,1:T(8,128)S(1)} %bitcast.283, f32[3,1024]{0,1:T(8,128)S(1)} %bitcast.285, f32[3,1024]{0,1:T(8,128)S(1)} %bitcast.281), kind=kLoop, calls=%fused_computation.2 | loop fusion | flops 18874368 | bytes 44077056 | tf_op jit(solution)/shard_map/convert_element_type | solution.py:221
  (150 shorter events, 441.3 us)
Async XLA Ops:
  7.2 154.3 %all-gather.2.cloned.1.call-start = ((), (), s32[]{:S(2)}) async-start(), calls=%async_computation.6 | async-start | bytes 10485760 | tf_op jit(solution)/shard_map/all_gather | solution.py:188
  8.7 20.8 %collective-permute-start = (bf16[1,2,3,1024]{3,1,2,0:T(2,128)(2,1)S(1)}, bf16[1,2,3,1024]{3,1,2,0:T(2,128)(2,1)S(1)}, u32[]{:S(2)}, u32[]{:S(2)}) collective-permute-start(bf16[1,2,3,1024]{3,1,2,0:T(2,128)(2,1)S(1)} %slice.194), channel_id=1, source_target_pairs={{0,4},{4,8},{8,12},{12,16},{16,20},{20,24},{24,28},{1,5},{5,9},{9,... | collective-permute-start | bytes 36872 | tf_op jit(solution)/shard_map/ppermute | solution.py:15
  29.0 12.1 %copy-start.7 = (f32[3,1,1024]{0,2,1:T(8,128)}, f32[3,1,1024]{0,2,1:T(8,128)S(1)}, u32[]{:S(2)}) copy-start(f32[3,1,1024]{0,2,1:T(8,128)S(1)} %copy.308) | copy-start | bytes 36868
  29.3 11.9 %copy-start.9 = (f32[3,1,1024]{0,2,1:T(8,128)}, f32[3,1,1024]{0,2,1:T(8,128)S(1)}, u32[]{:S(2)}) copy-start(f32[3,1,1024]{0,2,1:T(8,128)S(1)} %copy.310) | copy-start | bytes 36868
  29.5 11.7 %copy-start.11 = (f32[3,1,1024]{0,2,1:T(8,128)}, f32[3,1,1024]{0,2,1:T(8,128)S(1)}, u32[]{:S(2)}) copy-start(f32[3,1,1024]{0,2,1:T(8,128)S(1)} %copy.309) | copy-start | bytes 36868
  71.0 129.0 %all-to-all-start = ((bf16[3,1,1024,1024]{2,0,1,3:T(4,128)(2,1)}), bf16[3,1,1024,1024]{2,0,1,3:T(4,128)(2,1)}, u32[]{:S(2)}, u32[]{:S(2)}) async-start(bf16[3,1,1024,1024]{2,0,1,3:T(4,128)(2,1)} %fusion.92), calls=%async_computation | async-start | bytes 16777216 | tf_op jit(solution)/shard_map/all_to_all | solution.py:130
  86.7 329.0 %copy-start.13 = (f32[128,64]{1,0:T(8,128)}, f32[128,64]{1,0:T(8,128)S(1)}, u32[]{:S(2)}) copy-start(f32[128,64]{1,0:T(8,128)S(1)} %slice_negate_fusion) | copy-start | bytes 98308
  200.0 51.7 %all-to-all-start.2 = ((bf16[8,2,65536]{2,1,0:T(2,128)(2,1)}), bf16[8,2,65536]{2,1,0:T(2,128)(2,1)S(1)}, u32[]{:S(2)}, u32[]{:S(2)}) async-start(bf16[8,2,65536]{2,1,0:T(2,128)(2,1)} %reshape.366), calls=%async_computation.3 | async-start | bytes 4194304 | tf_op jit(solution)/shard_map/all_to_all | solution.py:130
  204.1 839.5 %reduce-scatter.2.cloned.1.call-start = ((), (), s32[]{:S(2)}) async-start(), calls=%async_computation.5 | async-start | bytes 10485760 | tf_op jit(solution)/shard_map/reduce_scatter | solution.py:178
  388.8 9.6 copy-start
  388.8 9.6 copy-start.15
  388.8 9.6 copy-start.17
  388.8 9.6 copy-start.19
  570.5 27.9 %slice-start = ((s8[8388608]{0:T(1024)(128)(4,1)}), s8[4194304]{0:T(1024)(128)(4,1)S(1)}, s32[]{:S(2)}) async-start(s8[8388608]{0:T(1024)(128)(4,1)} %bitcast.265), calls=%async_computation.7 | async-start | bytes 8388608
  584.5 13.8 %slice-start.1 = ((s8[8388608]{0:T(1024)(128)(4,1)}), s8[4194304]{0:T(1024)(128)(4,1)S(1)}, s32[]{:S(2)}) async-start(s8[8388608]{0:T(1024)(128)(4,1)} %bitcast.265), calls=%async_computation.8 | async-start | bytes 8388608
  611.4 31.7 %copy-start.16 = (f32[64,128]{1,0:T(8,128)S(1)}, f32[64,128]{1,0:T(8,128)}, u32[]{:S(2)}) copy-start(f32[64,128]{1,0:T(8,128)} %slice.271) | copy-start | bytes 98308
  611.4 31.7 %copy-start.18 = (f32[64,128]{1,0:T(8,128)S(1)}, f32[64,128]{1,0:T(8,128)}, u32[]{:S(2)}) copy-start(f32[64,128]{1,0:T(8,128)} %slice_negate_fusion.1) | copy-start | bytes 98308
  656.1 5.1 copy-start.21
  747.3 14.1 %copy-start.1 = (f32[1,128,128,128]{3,2,1,0:T(8,128)S(1)}, f32[1,128,128,128]{3,2,1,0:T(8,128)}, u32[]{:S(2)}) copy-start(f32[1,128,128,128]{3,2,1,0:T(8,128)} %get-tuple-element.52) | copy-start | bytes 25165828
  885.1 74.1 %all-to-all-start.3 = ((bf16[8,3,1,1024,128]{3,4,1,2,0:T(8,128)(2,1)}), bf16[8,3,1,1024,128]{3,4,1,2,0:T(8,128)(2,1)}, u32[]{:S(2)}, u32[]{:S(2)}) async-start(bf16[8,3,1,1024,128]{3,4,1,2,0:T(8,128)(2,1)} %fusion.125), calls=%async_computation.4 | async-start | bytes 12582912 | tf_op jit(solution)/shard_map/all_to_all | solution.py:136
  972.9 13.6 %collective-permute-start.1 = (bf16[1,2,3,1024]{3,1,2,0:T(2,128)(2,1)S(1)}, bf16[1,2,3,1024]{3,1,2,0:T(2,128)(2,1)S(1)}, u32[]{:S(2)}, u32[]{:S(2)}) collective-permute-start(bf16[1,2,3,1024]{3,1,2,0:T(2,128)(2,1)S(1)} %copy.275), channel_id=1, source_target_pairs={{4,0},{8,4},{12,8},{16,12},{20,16},{24,20},{28,24},{5,1},{9,5},{13... | collective-permute-start | bytes 36872 | tf_op jit(solution)/shard_map/ppermute | solution.py:15
  987.2 10.3 copy-start.8
  987.3 10.3 copy-start.10
  987.3 10.3 copy-start.12
  (8 other events, 29.8 us)
Sparse Core Ops, SparseCore 0:
  9.5 151.8 all-gather.1
  872.4 141.1 reduce-scatter.1
